TPU v7x, 32 devices: a whole 2x2x4 slice. The times are simulated.
32 devices in a mesh: vocab: 4 (over x, core), fsdp: 8 (over z, y).
Axes of the slice: x: 2, y: 2, z: 4, core: 2. Of those that a mesh axis runs over, the one named last changes fastest.
Arguments:
- hidden: bfloat16 [2, 384, 4096], P(None, 'fsdp'), may hold values from -1000 to 1000
- norm_gain: bfloat16 [4096], replicated, may hold values from 0.5 to 1.5
- labels: int32 [2, 384], P(None, 'fsdp'), may hold values from 0 to 65535
- head_weight: bfloat16 [4096, 65536], P(None, ('vocab', 'fsdp')), may hold values from -1 to 1
- head_ema: float32 [4096, 65536], P(None, ('vocab', 'fsdp')), may hold values from 1e-09 to 0.001
- gain_ema: float32 [4096], replicated, may hold values from 0.0001 to 0.03
Outputs:
- head_ema_new: float32 [4096, 65536], P(None, ('vocab', 'fsdp'))
- gain_ema_new: float32 [4096], replicated
All inputs are finite; a program needn't handle non-finite values.
Results may differ from a plain program's by a relative error of at most 0.00049.
Values may be sent and summed in bfloat16 or wider, within the bound.
A program may use at most 192 MiB of HBM per device.

v0:
```python
import jax
import jax.numpy as jnp
from jax import lax
from jax.sharding import PartitionSpec as P

BETA = 0.99
EPS = 1e-05


def on_device(hidden, norm_gain, labels, head_weight, head_ema, gain_ema):
    batches, own_rows, features = hidden.shape
    columns = head_weight.shape[1]
    column_ids = lax.iota(jnp.int32, columns)[None, :] + lax.axis_index(("vocab", "fsdp")) * columns
    gain_wide = norm_gain.astype(jnp.float32)
    wide = hidden.astype(jnp.float32)
    factor = lax.rsqrt(jnp.mean(wide * wide, axis=-1, keepdims=True) + EPS)
    scaled = (wide * factor * gain_wide).astype(jnp.bfloat16)
    count = batches * own_rows * lax.axis_size("fsdp")
    gradient = jnp.zeros((features, columns), jnp.float32)
    for batch in range(batches):
        batch_rows = scaled[batch]
        batch_labels = labels[batch]
        rows_all, labels_all = (
            lax.all_gather(batch_rows, "fsdp", axis=0, tiled=True),
            lax.all_gather(batch_labels, "fsdp", axis=0, tiled=True),
        )
        logits = jnp.dot(rows_all, head_weight, preferred_element_type=jnp.float32)
        local_top = jnp.max(logits, axis=1)
        row_top = lax.pmax(local_top, ("vocab", "fsdp"))
        local_total = jnp.sum(jnp.exp(logits - row_top[:, None]), axis=1)
        row_total = lax.psum(local_total, ("vocab", "fsdp"))
        chances = jnp.exp(logits - row_top[:, None]) / row_total[:, None]
        hits = (labels_all[:, None] == column_ids).astype(jnp.float32)
        slope = (chances - hits).astype(jnp.bfloat16)
        gradient = gradient + lax.dot_general(
            rows_all, slope, (((0,), (0,)), ((), ())), preferred_element_type=jnp.float32
        )
    head_new = BETA * head_ema + (1.0 - BETA) * gradient * gradient / count
    partial_sum = jnp.sum(head_weight.astype(jnp.float32) * gradient, axis=1)
    gain_grad = lax.psum(partial_sum, ("vocab", "fsdp")) / gain_wide
    gain_new = BETA * gain_ema + (1.0 - BETA) * gain_grad * gain_grad / count
    return (head_new, gain_new)


def solution(mesh):
    return jax.shard_map(
        on_device,
        mesh=mesh,
        in_specs=(
            P(None, "fsdp", None),
            P(),
            P(None, "fsdp"),
            P(None, ("vocab", "fsdp")),
            P(None, ("vocab", "fsdp")),
            P(),
        ),
        out_specs=(P(None, ("vocab", "fsdp")), P()),
        check_vma=False,
    )
```

profile of v0, /device:TPU:0, one launch (start us, length us, event | category | flops | bytes accessed | tf_op | source)
XLA Modules:
  0.0 369.3 jit_solution(13150943076576442699)
XLA Ops:
  7.2 0.0 all-gather.7.cloned.1.call-start
  7.2 1.4 fusion.11
  8.6 0.7 convert_element_type.25
  9.3 1.4 fusion.13
  10.7 0.9 fusion.24
  11.6 0.0 all-gather.7.cloned.1.call-update
  11.7 0.0 all-gather.9.cloned.1.call-start
  11.7 0.7 all-gather.9.cloned.1.call-update
  12.4 21.0 %copy.9 = bf16[4096,2048]{0,1:T(8,128)(2,1)} copy(bf16[4096,2048]{1,0:T(8,128)(2,1)} %param.9) | data formatting | bytes 33554432 | tf_op args[3]
  33.4 0.0 copy-start.3
  33.4 0.0 copy-start.2
  33.4 31.2 %copy.8 = f32[4096,2048]{0,1:T(8,128)} copy(f32[4096,2048]{1,0:T(8,128)} %param.10) | data formatting | bytes 67108864 | tf_op args[4]
  64.6 0.0 copy-done.3
  64.6 0.6 dynamic-slice
  65.8 0.0 copy-done.2
  65.9 0.1 bitcast_dynamic-update-slice_fusion.1
  66.0 0.1 bitcast_dynamic-update-slice_fusion
  66.0 13.1 %all-reduce.2 = (s32[384]{0:T(512)S(1)}, s32[384]{0:T(512)S(1)}) all-reduce(s32[384]{0:T(512)S(1)} %bitcast_dynamic-update-slice_fusion.1, s32[384]{0:T(512)S(1)} %bitcast_dynamic-update-slice_fusion), channel_id=3, replica_groups=mesh['vocab'=4,'fsdp'=8] {'fsdp'}, use_global_device_ids=true, to_apply=%add | all-reduce | flops 768 | bytes 6144
  79.1 0.0 all-gather.7.cloned.1.call-done
  79.1 11.5 %fusion.25 = (f32[384]{0:T(512)S(1)}, f32[384,2048]{1,0:T(8,128)S(1)}) fusion(bf16[4096,2048]{1,0:T(8,128)(2,1)} %param.9, bf16[1,384,4096]{2,1,0:T(8,128)(2,1)} %all-gather.7.cloned.1.call-done), kind=kOutput, calls=%fused_computation.39 | convolution fusion | flops 6443236864 | bytes 23070208 | tf_op jit(solution)/shard_map/dot_general | solution.py:27
  90.6 44.9 %all-gather.9.cloned.1.call-done = bf16[1,384,4096]{2,1,0:T(8,128)(2,1)} async-done(((bf16[1,48,4096]{2,1,0:T(8,128)(2,1)}), bf16[1,384,4096]{2,1,0:T(8,128)(2,1)}) %all-gather.9.cloned.1.call-update) | async-done | bytes 3145744 | tf_op jit(solution)/shard_map/all_gather | solution.py:24
  135.5 12.3 %fusion.26 = (f32[384]{0:T(512)S(1)}, f32[384,2048]{1,0:T(8,128)}) fusion(bf16[4096,2048]{1,0:T(8,128)(2,1)} %param.9, bf16[1,384,4096]{2,1,0:T(8,128)(2,1)} %all-gather.9.cloned.1.call-done), kind=kOutput, calls=%fused_computation.40 | convolution fusion | flops 6443236864 | bytes 23070208 | tf_op jit(solution)/shard_map/dot_general | solution.py:27
  147.8 39.2 %all-reduce.4 = (f32[384]{0:T(512)S(1)}, f32[384]{0:T(512)S(1)}) all-reduce(f32[384]{0:T(512)S(1)} %get-tuple-element.14, f32[384]{0:T(512)S(1)} %get-tuple-element.16), channel_id=1, replica_groups=mesh['vocab'=4,'fsdp'=8] {'vocab','fsdp'}, use_global_device_ids=true, to_apply=%region_2.0 | all-reduce | flops 768 | bytes 6144 | tf_op jit(solution)/shard_map/pmax | solution.py:29
  187.0 2.9 fusion.9
  189.9 40.1 %all-reduce.3 = (f32[384]{0:T(512)S(1)}, f32[384]{0:T(512)S(1)}) all-reduce(f32[384]{0:T(512)S(1)} %get-tuple-element.18, f32[384]{0:T(512)S(1)} %get-tuple-element.19), channel_id=1, replica_groups=mesh['vocab'=4,'fsdp'=8] {'vocab','fsdp'}, use_global_device_ids=true, to_apply=%region_4.0 | all-reduce | flops 768 | bytes 6144 | tf_op jit(solution)/shard_map/psum | solution.py:31
  229.9 17.4 %fusion.5 = f32[4096,2048]{0,1:T(8,128)} fusion(bf16[1,384,4096]{2,1,0:T(8,128)(2,1)} %all-gather.7.cloned.1.call-done, f32[384,2048]{1,0:T(8,128)S(1)} %get-tuple-element.15, s32[2048]{0:T(1024)S(1)} %iota_add_fusion, f32[384]{0:T(512)S(1)} %get-tuple-element.6, f32[384]{0:T(512)S(1)} %get-tuple-element.8, s32[384]{0:T(512)S(1)} %get-tuple-element.4), kind=kOutput, calls=%fused_computation.8 | convolution fusion | flops 6447169536 | bytes 39858688 | tf_op jit(solution)/shard_map/dot_general | solution.py:35
  247.3 41.1 %multiply_reduce_fusion = (f32[4096]{0:T(1024)S(1)}, f32[4096,2048]{0,1:T(8,128)}) fusion(bf16[4096,2048]{0,1:T(8,128)(2,1)} %copy.9, f32[4096,2048]{0,1:T(8,128)} %copy.8, f32[4096,2048]{0,1:T(8,128)} %fusion.5, f32[384,2048]{1,0:T(8,128)} %get-tuple-element.17, f32[384]{0:T(512)S(1)} %get-tuple-element.7, f32[384]{0:T(512)S(1)} %get-tuple-element.9, ...), kind=kOutput, calls=%fused_computation.3 | convolution fusion | flops 6522662912 | bytes 123761152 | tf_op jit(solution)/shard_map/dot_general | solution.py:35
  288.4 40.1 %psum.23 = f32[4096]{0:T(1024)S(1)} all-reduce(f32[4096]{0:T(1024)S(1)} %get-tuple-element.10), channel_id=1, replica_groups=mesh['vocab'=4,'fsdp'=8] {'vocab','fsdp'}, use_global_device_ids=true, to_apply=%region_10.0 | all-reduce | flops 4096 | bytes 32768 | tf_op jit(solution)/shard_map/psum | solution.py:40
  328.5 0.0 copy-start
  328.5 0.0 copy-start.1
  328.5 33.4 %copy.10 = f32[4096,2048]{1,0:T(8,128)} copy(f32[4096,2048]{0,1:T(8,128)} %get-tuple-element.11) | data formatting | bytes 67108864
  361.9 0.0 copy-done
  361.9 0.0 copy-done.1
  361.9 0.6 fusion.23
  (4 shorter events, 0.0 us)
Async XLA Ops:
  7.2 72.0 %all-gather.7.cloned.1.call-start = ((), (), s32[]{:S(2)}) async-start(), calls=%async_computation | async-start | bytes 3538944 | tf_op jit(solution)/shard_map/all_gather | solution.py:24
  11.7 123.8 %all-gather.9.cloned.1.call-start = ((), (), s32[]{:S(2)}) async-start(), calls=%async_computation.1 | async-start | bytes 3538944 | tf_op jit(solution)/shard_map/all_gather | solution.py:24
  33.4 31.2 %copy-start.3 = (u32[32]{0:T(128)S(1)}, u32[32]{0:T(128)}, u32[]{:S(2)}) copy-start(u32[32]{0:T(128)} %constant.34) | copy-start | bytes 388
  33.4 32.4 %copy-start.2 = (s32[2,48]{1,0:T(2,128)S(1)}, s32[2,48]{1,0:T(2,128)}, u32[]{:S(2)}) copy-start(s32[2,48]{1,0:T(2,128)} %param.8) | copy-start | bytes 1156
  328.5 33.4 %copy-start = (bf16[4096]{0:T(1024)(128)(2,1)S(1)}, bf16[4096]{0:T(1024)(128)(2,1)}, u32[]{:S(2)}) copy-start(bf16[4096]{0:T(1024)(128)(2,1)} %param.7) | copy-start | bytes 24580
  328.5 33.4 %copy-start.1 = (f32[4096]{0:T(1024)S(1)}, f32[4096]{0:T(1024)}, u32[]{:S(2)}) copy-start(f32[4096]{0:T(1024)} %param.11) | copy-start | bytes 49156
Sparse Core Ops, SparseCore 0:
  11.8 62.7 all-gather.6
  76.7 58.7 all-gather.8
where the time goes:
time: 371 us; the launch traced here: 369 us
  blocking collectives  132 us (36%)
  local copies, waits for them, and re-layouts  87.3 us (24%)
  matrix products  82.3 us (22%)
  waiting for transfers between devices  45.6 us (12%)
  between operations  14.7 us (4%)
  other arithmetic  6.97 us (2%)
    unnamed x16, local copies, waits for them, and re-layouts  86.3 us
    dot_general x2, matrix products, on_device(): lax.dot_general(rows_all, slope, (((0,), (0,)), ((), ())), preferred_elem...  58.5 us
    all_gather x2, waiting for transfers between devices, on_device(): lax.all_gather(batch_rows, 'fsdp', axis=0, tiled=True)  44.9 us
    psum x1, blocking collectives, on_device(): row_total = lax.psum(local_total, ('vocab', 'fsdp'))  40.1 us
    psum x1, blocking collectives, on_device(): gain_grad = lax.psum(partial_sum, ('vocab', 'fsdp')) / gain_wide  40.1 us
    pmax x1, blocking collectives, on_device(): row_top = lax.pmax(local_top, ('vocab', 'fsdp'))  39.2 us
    dot_general x2, matrix products, on_device(): logits = jnp.dot(rows_all, head_weight, preferred_element_type=jnp.float32)  23.8 us
    unnamed x1, blocking collectives  13.1 us
  transfers between devices with their start and end apart: 2, of which 1 were waited for; matrix products, arithmetic and copies ran while one was open for 17% of the time, Pallas kernels for 0%

commit v1 on v0

--- a/solution.py
+++ b/solution.py
@@ -1,3 +1,4 @@
+import functools
 import jax
 import jax.numpy as jnp
 from jax import lax
@@ -5,6 +6,15 @@
 
 BETA = 0.99
 EPS = 1e-05
+
+
+def bind_the_racks(x0, axis_key, mesh_dim):
+    for ii in (axis_key, mesh_dim):
+        x0 = lax.psum(x0, ii)
+    return x0
+
+
+link_screen = functools.partial(bind_the_racks, axis_key="fsdp", mesh_dim="vocab")
 
 
 def on_device(hidden, norm_gain, labels, head_weight, head_ema, gain_ema):
@@ -37,7 +47,7 @@
         )
     head_new = BETA * head_ema + (1.0 - BETA) * gradient * gradient / count
     partial_sum = jnp.sum(head_weight.astype(jnp.float32) * gradient, axis=1)
-    gain_grad = lax.psum(partial_sum, ("vocab", "fsdp")) / gain_wide
+    gain_grad = link_screen(partial_sum) / gain_wide
     gain_new = BETA * gain_ema + (1.0 - BETA) * gain_grad * gain_grad / count
     return (head_new, gain_new)
 

time: 371 us -> 378 us (1.019)
  blocking collectives: 132 us -> 139 us
    psum x1 -> x2, blocking collectives: 40.1 us -> 46.8 us  [bind_the_racks(): x0 = lax.psum(x0, ii)]
where the time goes in v1:
time: 378 us; the launch traced here: 376 us
  blocking collectives  139 us (37%)
  local copies, waits for them, and re-layouts  87.3 us (23%)
  matrix products  82.3 us (22%)
  waiting for transfers between devices  45.6 us (12%)
  between operations  14.8 us (4%)
  other arithmetic  6.97 us (2%)
    unnamed x16, local copies, waits for them, and re-layouts  86.3 us
    dot_general x2, matrix products, on_device(): lax.dot_general(rows_all, slope, (((0,), (0,)), ((), ())), preferred_elem...  58.5 us
    psum x2, blocking collectives, bind_the_racks(): x0 = lax.psum(x0, ii)  46.8 us
    all_gather x2, waiting for transfers between devices, on_device(): lax.all_gather(batch_rows, 'fsdp', axis=0, tiled=True)  44.9 us
    psum x1, blocking collectives, on_device(): row_total = lax.psum(local_total, ('vocab', 'fsdp'))  40.1 us
    pmax x1, blocking collectives, on_device(): row_top = lax.pmax(local_top, ('vocab', 'fsdp'))  39.2 us
    dot_general x2, matrix products, on_device(): logits = jnp.dot(rows_all, head_weight, preferred_element_type=jnp.float32)  23.8 us
    unnamed x1, blocking collectives  13.1 us
  transfers between devices with their start and end apart: 2, of which 1 were waited for; matrix products, arithmetic and copies ran while one was open for 17% of the time, Pallas kernels for 0%

profile of v1, /device:TPU:0, one launch (start us, length us, event | category | flops | bytes accessed | tf_op | source)
XLA Modules:
  0.0 376.0 jit_solution(9877657261390933105)
XLA Ops:
  7.2 0.0 all-gather.7.cloned.1.call-start
  7.2 1.4 fusion.11
  8.6 0.7 convert_element_type.25
  9.3 1.4 fusion.13
  10.7 0.9 fusion.24
  11.6 0.0 all-gather.7.cloned.1.call-update
  11.7 0.0 all-gather.9.cloned.1.call-start
  11.7 0.7 all-gather.9.cloned.1.call-update
  12.4 21.0 %copy.9 = bf16[4096,2048]{0,1:T(8,128)(2,1)} copy(bf16[4096,2048]{1,0:T(8,128)(2,1)} %param.9) | data formatting | bytes 33554432 | tf_op args[3]
  33.4 0.0 copy-start.3
  33.4 0.0 copy-start.2
  33.4 31.2 %copy.8 = f32[4096,2048]{0,1:T(8,128)} copy(f32[4096,2048]{1,0:T(8,128)} %param.10) | data formatting | bytes 67108864 | tf_op args[4]
  64.6 0.0 copy-done.3
  64.6 0.6 dynamic-slice
  65.8 0.0 copy-done.2
  65.9 0.1 bitcast_dynamic-update-slice_fusion.1
  66.0 0.1 bitcast_dynamic-update-slice_fusion
  66.0 13.1 %all-reduce.2 = (s32[384]{0:T(512)S(1)}, s32[384]{0:T(512)S(1)}) all-reduce(s32[384]{0:T(512)S(1)} %bitcast_dynamic-update-slice_fusion.1, s32[384]{0:T(512)S(1)} %bitcast_dynamic-update-slice_fusion), channel_id=3, replica_groups=mesh['vocab'=4,'fsdp'=8] {'fsdp'}, use_global_device_ids=true, to_apply=%add | all-reduce | flops 768 | bytes 6144
  79.1 0.0 all-gather.7.cloned.1.call-done
  79.1 11.5 %fusion.25 = (f32[384]{0:T(512)S(1)}, f32[384,2048]{1,0:T(8,128)S(1)}) fusion(bf16[4096,2048]{1,0:T(8,128)(2,1)} %param.9, bf16[1,384,4096]{2,1,0:T(8,128)(2,1)} %all-gather.7.cloned.1.call-done), kind=kOutput, calls=%fused_computation.39 | convolution fusion | flops 6443236864 | bytes 23070208 | tf_op jit(solution)/shard_map/dot_general | solution.py:37
  90.6 44.9 %all-gather.9.cloned.1.call-done = bf16[1,384,4096]{2,1,0:T(8,128)(2,1)} async-done(((bf16[1,48,4096]{2,1,0:T(8,128)(2,1)}), bf16[1,384,4096]{2,1,0:T(8,128)(2,1)}) %all-gather.9.cloned.1.call-update) | async-done | bytes 3145744 | tf_op jit(solution)/shard_map/all_gather | solution.py:34
  135.5 12.3 %fusion.26 = (f32[384]{0:T(512)S(1)}, f32[384,2048]{1,0:T(8,128)}) fusion(bf16[4096,2048]{1,0:T(8,128)(2,1)} %param.9, bf16[1,384,4096]{2,1,0:T(8,128)(2,1)} %all-gather.9.cloned.1.call-done), kind=kOutput, calls=%fused_computation.40 | convolution fusion | flops 6443236864 | bytes 23070208 | tf_op jit(solution)/shard_map/dot_general | solution.py:37
  147.8 39.2 %all-reduce.4 = (f32[384]{0:T(512)S(1)}, f32[384]{0:T(512)S(1)}) all-reduce(f32[384]{0:T(512)S(1)} %get-tuple-element.14, f32[384]{0:T(512)S(1)} %get-tuple-element.16), channel_id=1, replica_groups=mesh['vocab'=4,'fsdp'=8] {'vocab','fsdp'}, use_global_device_ids=true, to_apply=%region_2.0 | all-reduce | flops 768 | bytes 6144 | tf_op jit(solution)/shard_map/pmax | solution.py:39
  187.0 2.9 fusion.9
  189.9 40.1 %all-reduce.3 = (f32[384]{0:T(512)S(1)}, f32[384]{0:T(512)S(1)}) all-reduce(f32[384]{0:T(512)S(1)} %get-tuple-element.18, f32[384]{0:T(512)S(1)} %get-tuple-element.19), channel_id=1, replica_groups=mesh['vocab'=4,'fsdp'=8] {'vocab','fsdp'}, use_global_device_ids=true, to_apply=%region_4.0 | all-reduce | flops 768 | bytes 6144 | tf_op jit(solution)/shard_map/psum | solution.py:41
  229.9 17.4 %fusion.5 = f32[4096,2048]{0,1:T(8,128)} fusion(bf16[1,384,4096]{2,1,0:T(8,128)(2,1)} %all-gather.7.cloned.1.call-done, f32[384,2048]{1,0:T(8,128)S(1)} %get-tuple-element.15, s32[2048]{0:T(1024)S(1)} %iota_add_fusion, f32[384]{0:T(512)S(1)} %get-tuple-element.6, f32[384]{0:T(512)S(1)} %get-tuple-element.8, s32[384]{0:T(512)S(1)} %get-tuple-element.4), kind=kOutput, calls=%fused_computation.8 | convolution fusion | flops 6447169536 | bytes 39858688 | tf_op jit(solution)/shard_map/dot_general | solution.py:45
  247.3 41.1 %multiply_reduce_fusion = (f32[4096]{0:T(1024)S(1)}, f32[4096,2048]{0,1:T(8,128)}) fusion(bf16[4096,2048]{0,1:T(8,128)(2,1)} %copy.9, f32[4096,2048]{0,1:T(8,128)} %copy.8, f32[4096,2048]{0,1:T(8,128)} %fusion.5, f32[384,2048]{1,0:T(8,128)} %get-tuple-element.17, f32[384]{0:T(512)S(1)} %get-tuple-element.7, f32[384]{0:T(512)S(1)} %get-tuple-element.9, ...), kind=kOutput, calls=%fused_computation.3 | convolution fusion | flops 6522662912 | bytes 123761152 | tf_op jit(solution)/shard_map/dot_general | solution.py:45
  288.4 36.5 %psum.30 = f32[4096]{0:T(1024)S(1)} all-reduce(f32[4096]{0:T(1024)S(1)} %get-tuple-element.10), channel_id=1, replica_groups=mesh['vocab'=4,'fsdp'=8] {'fsdp'}, use_global_device_ids=true, to_apply=%region_10.0 | all-reduce | flops 4096 | bytes 32768 | tf_op jit(solution)/shard_map/psum | solution.py:13
  325.0 10.2 %psum.31 = f32[4096]{0:T(1024)S(1)} all-reduce(f32[4096]{0:T(1024)S(1)} %psum.30), channel_id=1, replica_groups=mesh['vocab'=4,'fsdp'=8] {'vocab'}, use_global_device_ids=true, to_apply=%region_11.0 | all-reduce | flops 4096 | bytes 32768 | tf_op jit(solution)/shard_map/psum | solution.py:13
  335.2 0.0 copy-start
  335.2 0.0 copy-start.1
  335.2 33.4 %copy.10 = f32[4096,2048]{1,0:T(8,128)} copy(f32[4096,2048]{0,1:T(8,128)} %get-tuple-element.11) | data formatting | bytes 67108864
  368.6 0.0 copy-done
  368.6 0.0 copy-done.1
  368.6 0.6 fusion.23
  (4 shorter events, 0.0 us)
Async XLA Ops:
  7.2 72.0 %all-gather.7.cloned.1.call-start = ((), (), s32[]{:S(2)}) async-start(), calls=%async_computation | async-start | bytes 3538944 | tf_op jit(solution)/shard_map/all_gather | solution.py:34
  11.7 123.8 %all-gather.9.cloned.1.call-start = ((), (), s32[]{:S(2)}) async-start(), calls=%async_computation.1 | async-start | bytes 3538944 | tf_op jit(solution)/shard_map/all_gather | solution.py:34
  33.4 31.2 %copy-start.3 = (u32[32]{0:T(128)S(1)}, u32[32]{0:T(128)}, u32[]{:S(2)}) copy-start(u32[32]{0:T(128)} %constant.34) | copy-start | bytes 388
  33.4 32.4 %copy-start.2 = (s32[2,48]{1,0:T(2,128)S(1)}, s32[2,48]{1,0:T(2,128)}, u32[]{:S(2)}) copy-start(s32[2,48]{1,0:T(2,128)} %param.8) | copy-start | bytes 1156
  335.2 33.4 %copy-start = (bf16[4096]{0:T(1024)(128)(2,1)S(1)}, bf16[4096]{0:T(1024)(128)(2,1)}, u32[]{:S(2)}) copy-start(bf16[4096]{0:T(1024)(128)(2,1)} %param.7) | copy-start | bytes 24580
  335.2 33.4 %copy-start.1 = (f32[4096]{0:T(1024)S(1)}, f32[4096]{0:T(1024)}, u32[]{:S(2)}) copy-start(f32[4096]{0:T(1024)} %param.11) | copy-start | bytes 49156
Sparse Core Ops, SparseCore 0:
  11.8 62.7 all-gather.6
  76.7 58.7 all-gather.8
